TPU v7x, 256 devices: a whole 4x4x8 slice. The times are simulated.
256 devices in a mesh: gx: 8 (over x_hi, y), gy: 16 (over z, x_lo), af: 2 (over core).
Axes of the slice: x: 4 (x_hi: 2, x_lo: 2; x = x_hi * 2 + x_lo), y: 4, z: 8, core: 2. Of those that a mesh axis runs over, the one named last changes fastest.
Arguments:
- model: float32 [256, 512, 128], P('gx', 'gy'), may hold values from 0.5 to 2
- freq_sq: float32 [4], P('af'), may hold values from 0.5 to 3
- source: float32 [4, 2, 256, 512, 128], P('af', None, 'gx', 'gy'), may hold values from -20 to 20
- observed: float32 [4, 2, 256, 512], P('af', None, 'gx', 'gy'), may hold values from -6 to 6
- receiver_depth: int32 [256, 512], P('gx', 'gy'), may hold values from 0 to 3
Outputs:
- wavefield: float32 [4, 2, 256, 512, 128], P('af', None, 'gx', 'gy')
- gradient: float32 [256, 512, 128], P('gx', 'gy')
Inputs may be any that keep to these rules, and one draw needn't show every extreme that they name: `receiver_depth`: every surface column holds one receiver, at the given depth index.
All inputs are finite; a program needn't handle non-finite values.
Results may differ from a plain program's by a relative error of at most 0.00012.
Values sent between devices are 32-bit elements; how exact they have to be, the bound alone decides.
A program may use at most 64 MiB of HBM per device.

v0:
```python
import jax
import jax.numpy as jnp
from jax import lax
from jax.sharding import PartitionSpec as P

ITERS = 2
attenuation = 0.2
penalty = 4.0


def padded_2(cells, sides, width):
    for axis, dim in sides:
        count = lax.axis_size(axis)
        ends = count - 1
        head = lax.slice_in_dim(cells, 0, width, axis=dim)
        tail = lax.slice_in_dim(cells, cells.shape[dim] - width, cells.shape[dim], axis=dim)
        cells = jnp.concatenate(
            [
                lax.ppermute(tail, axis, [(i, (i + 1) % count) for i in range(ends)]),
                cells,
                lax.ppermute(head, axis, [((i + 1) % count, i) for i in range(ends)]),
            ],
            axis=dim,
        )
    return cells


def stencil_sum(padded):
    center = padded[:, :, 1:-1, 1:-1]
    total = padded[:, :, 2:, 1:-1] + padded[:, :, :-2, 1:-1]
    total = total + padded[:, :, 1:-1, 2:] + padded[:, :, 1:-1, :-2]
    upper = jnp.pad(center[..., 1:], ((0, 0), (0, 0), (0, 0), (0, 0), (0, 1)))
    lower = jnp.pad(center[..., :-1], ((0, 0), (0, 0), (0, 0), (0, 0), (1, 0)))
    return (center, total + upper + lower)


def apply_coef(coef_real, coef_imag, field, sign):
    real_part = coef_real * field[:, 0] - sign * coef_imag * field[:, 1]
    imag_part = coef_real * field[:, 1] + sign * coef_imag * field[:, 0]
    return jnp.stack([real_part, imag_part], axis=1)


def beside(field):
    padded = padded_2(field, (("gx", 2), ("gy", 3)), 1)
    center, total = stencil_sum(padded)
    return total


def inner(left, right):
    return jnp.sum(left * right, axis=(1, 2, 3, 4))


def expand(values):
    return values[:, None, None, None, None]


def on_device(model, freq_sq, source, observed, receiver_depth):
    squared = freq_sq[:, None, None, None]
    coef_real = 6.0 - squared * model[None]
    coef_imag = attenuation * squared * model[None]
    levels = lax.broadcasted_iota(jnp.int32, model.shape, 2)
    onehot = (levels == receiver_depth[:, :, None]).astype(jnp.float32)
    weights = penalty * onehot

    def forward(field):
        return apply_coef(coef_real, coef_imag, field, 1.0) - beside(field)

    def adjoint(field):
        return apply_coef(coef_real, coef_imag, field, -1.0) - beside(field)

    rhs = adjoint(source) + weights * observed[:, :, :, :, None]
    field = jnp.zeros_like(rhs)
    resid = rhs

    def squares(values):
        return lax.psum(inner(values, values), ("gx", "gy"))

    direction = rhs
    norm_now = squares(resid)
    for sweep in range(ITERS):
        image = adjoint(forward(direction)) + weights * direction
        alpha = norm_now / lax.psum(inner(direction, image), ("gx", "gy"))
        field = field + expand(alpha) * direction
        resid = resid - expand(alpha) * image
        norm_next = squares(resid)
        direction = resid + expand(norm_next / norm_now) * direction
        norm_now = norm_next
    misfit = forward(field) - source
    deriv_real = -squared
    deriv_imag = attenuation * squared
    wave_real = deriv_real * field[:, 0] - deriv_imag * field[:, 1]
    wave_imag = deriv_real * field[:, 1] + deriv_imag * field[:, 0]
    local_terms = jnp.sum(wave_real * misfit[:, 0] + wave_imag * misfit[:, 1], axis=0)
    gradient = lax.psum(local_terms, "af")
    return (field, gradient)


def solution(mesh):
    in_specs = (
        P("gx", "gy", None),
        P("af"),
        P("af", None, "gx", "gy", None),
        P("af", None, "gx", "gy"),
        P("gx", "gy"),
    )
    out_specs = (P("af", None, "gx", "gy", None), P("gx", "gy", None))
    return jax.shard_map(
        on_device, mesh=mesh, in_specs=in_specs, out_specs=out_specs, check_vma=False
    )
```

profile of v0, /device:TPU:1, one launch (start us, length us, event | category | flops | bytes accessed | tf_op | source)
XLA Modules:
  0.0 1227.7 jit_solution(6360724979951832859)
XLA Ops:
  7.2 0.9 fusion.80
  8.2 1.3 collective-permute-start
  9.6 4.8 collective-permute-start.1
  14.4 2.8 copy.48
  17.5 2.8 fusion.79
  20.3 1.8 fusion.48
  22.2 0.7 pad_maximum_fusion.62
  22.9 1.3 collective-permute-start.2
  24.2 4.0 collective-permute-start.3
  28.4 0.9 copy.58
  29.4 1.4 collective-permute-done.3
  30.8 7.4 fusion.45
  38.3 1.3 collective-permute-start.4
  39.6 4.0 collective-permute-start.5
  43.6 0.8 fusion.77
  44.4 0.5 collective-permute-done.5
  44.9 1.3 collective-permute-start.6
  46.2 4.3 collective-permute-start.7
  51.0 1.1 collective-permute-done.7
  52.0 2.1 fusion.38
  54.3 1.3 collective-permute-start.8
  55.6 4.6 collective-permute-start.9
  60.2 0.7 fusion.76
  61.0 0.5 collective-permute-done.9
  61.5 1.3 collective-permute-start.10
  62.8 4.9 collective-permute-start.11
  67.7 0.4 fusion.50
  68.2 1.1 collective-permute-done.11
  69.3 4.1 multiply_reduce_fusion.1
  73.4 305.5 %all-reduce.12 = (f32[2]{0:T(128)S(1)}, f32[2]{0:T(128)S(1)}) all-reduce(f32[2]{0:T(128)S(1)} %get-tuple-element.7, f32[2]{0:T(128)S(1)} %get-tuple-element.6), channel_id=1, replica_groups=mesh['gx'=8,'gy'=16,'af'=2] {'gx','gy'}, use_global_device_ids=true, to_apply=%region_1.2 | all-reduce | flops 4 | bytes 32 | tf_op jit(solution)/shard_map/psum | solution.py:76
  378.9 2.1 multiply_reduce_fusion
  381.0 286.8 %psum.37 = f32[2]{0:T(128)S(1)} all-reduce(f32[2]{0:T(128)S(1)} %multiply_reduce_fusion), channel_id=1, replica_groups=mesh['gx'=8,'gy'=16,'af'=2] {'gx','gy'}, use_global_device_ids=true, to_apply=%region_5.6 | all-reduce | flops 2 | bytes 16 | tf_op jit(solution)/shard_map/psum | solution.py:76
  667.8 2.2 multiply_add_fusion.1
  670.1 1.3 collective-permute-start.12
  671.4 4.2 collective-permute-start.13
  675.5 0.7 fusion.73
  676.7 1.3 collective-permute-start.14
  678.0 4.1 collective-permute-start.15
  682.5 1.1 collective-permute-done.15
  683.6 2.0 fusion.25
  685.7 1.3 collective-permute-start.16
  687.0 4.3 collective-permute-start.17
  691.3 0.7 fusion.71
  692.1 0.5 collective-permute-done.17
  692.7 1.3 collective-permute-start.18
  694.0 4.9 collective-permute-start.19
  698.9 0.4 fusion.52
  699.3 1.5 collective-permute-done.19
  700.8 3.0 fusion.19
  703.8 289.7 %psum.38 = f32[2]{0:T(128)S(1)} all-reduce(f32[2]{0:T(128)S(1)} %fusion.19), channel_id=1, replica_groups=mesh['gx'=8,'gy'=16,'af'=2] {'gx','gy'}, use_global_device_ids=true, to_apply=%region_7.8 | all-reduce | flops 2 | bytes 16 | tf_op jit(solution)/shard_map/psum | solution.py:82
  993.6 2.2 multiply_add_fusion
  995.8 0.4 fusion.58
  996.3 0.7 fusion.69
  997.0 1.3 collective-permute-start.20
  998.3 4.0 collective-permute-start.21
  1002.5 1.1 collective-permute-done.21
  1003.6 1.3 collective-permute-start.22
  1005.0 4.1 collective-permute-start.23
  1009.5 1.1 collective-permute-done.23
  1010.6 2.7 fusion.10
  1013.2 1.4 fusion.62
  1014.7 4.1 copy.70
  1018.8 199.9 %all-reduce.15.cloned.1.call-done = f32[32,32,128]{2,0,1:T(8,128)} async-done(((f32[32,32,128]{2,0,1:T(8,128)}), f32[32,32,128]{2,0,1:T(8,128)}) %all-reduce.15.cloned.1.call-update) | async-done | bytes 524304 | tf_op jit(solution)/shard_map/psum | solution.py:94
  1218.7 2.1 copy.71
  (53 shorter events, 3.2 us)
Async XLA Ops:
  7.2 1211.5 %all-reduce.15.cloned.1.call-start = ((), (), s32[]{:S(2)}) async-start(), calls=%async_computation | async-start | bytes 1048576 | tf_op jit(solution)/shard_map/psum | solution.py:94
  8.2 14.1 %collective-permute-start = (f32[2,2,1,32,128]{4,2,3,0,1:T(1,128)S(1)}, f32[2,2,1,32,128]{4,2,3,0,1:T(1,128)S(1)}, u32[]{:S(2)}, u32[]{:S(2)}) collective-permute-start(f32[2,2,1,32,128]{4,2,3,0,1:T(1,128)S(1)} %copy.50), channel_id=1, source_target_pairs={{32,0},{64,32},{96,64},{128,96},{160,128},{192,160},{224,192},{33,... | collective-permute-start | bytes 196616 | tf_op jit(solution)/shard_map/ppermute | solution.py:21
  9.6 7.6 copy-start.5
  9.6 7.6 copy-start.4
  9.6 12.7 %collective-permute-start.1 = (f32[2,2,1,32,128]{4,2,3,0,1:T(1,128)S(1)}, f32[2,2,1,32,128]{4,2,3,0,1:T(1,128)S(1)}, u32[]{:S(2)}, u32[]{:S(2)}) collective-permute-start(f32[2,2,1,32,128]{4,2,3,0,1:T(1,128)S(1)} %copy.52), channel_id=1, source_target_pairs={{0,32},{32,64},{64,96},{96,128},{128,160},{160,192},{192,224},{1,3... | collective-permute-start | bytes 196616 | tf_op jit(solution)/shard_map/ppermute | solution.py:19
  17.2 5.0 copy-start.2
  20.3 1.8 copy-start.6
  22.9 6.4 collective-permute-start.2
  24.2 6.6 collective-permute-start.3
  38.3 6.1 collective-permute-start.4
  39.6 5.3 collective-permute-start.5
  44.9 6.0 collective-permute-start.6
  46.2 5.8 collective-permute-start.7
  54.3 6.7 collective-permute-start.8
  55.6 5.9 collective-permute-start.9
  61.5 6.6 collective-permute-start.10
  62.8 6.5 collective-permute-start.11
  670.0 30.9 %copy-start.1 = (f32[2,2,32,32,128]{4,2,3,0,1:T(8,128)}, f32[2,2,32,32,128]{4,2,3,0,1:T(8,128)S(1)}, u32[]{:S(2)}) copy-start(f32[2,2,32,32,128]{4,2,3,0,1:T(8,128)S(1)} %multiply_add_fusion.1) | copy-start | bytes 6291460
  670.1 6.2 collective-permute-start.12
  671.4 5.3 collective-permute-start.13
  676.7 5.8 collective-permute-start.14
  678.0 5.6 collective-permute-start.15
  685.7 6.4 collective-permute-start.16
  687.0 5.6 collective-permute-start.17
  692.7 6.6 collective-permute-start.18
  694.0 6.8 collective-permute-start.19
  995.7 17.5 %copy-start = (f32[2,2,32,32,128]{4,2,3,0,1:T(8,128)}, f32[2,2,32,32,128]{4,2,3,0,1:T(8,128)S(1)}, u32[]{:S(2)}) copy-start(f32[2,2,32,32,128]{4,2,3,0,1:T(8,128)S(1)} %multiply_add_fusion) | copy-start | bytes 6291460
  997.0 5.5 collective-permute-start.20
  998.3 5.3 collective-permute-start.21
  1003.6 5.8 collective-permute-start.22
  1004.9 5.6 copy-start.3
  1005.0 5.6 collective-permute-start.23
Sparse Core Ops, SparseCore 0:
  1014.8 203.8 all-reduce.14
where the time goes:
time: 1230 us
  blocking collectives  882 us (72%)
  waiting for transfers between devices  210 us (17%)
  starting transfers between devices  67.7 us (6%)
  other arithmetic  34.7 us (3%)
  local copies, waits for them, and re-layouts  18.4 us (1%)
  between operations  14.6 us (1%)
    psum x2, blocking collectives, squares(): return lax.psum(inner(values, values), ('gx', 'gy'))  592 us
    psum x1, blocking collectives, on_device(): alpha = norm_now / lax.psum(inner(direction, image), ('gx', 'gy'))  290 us
    psum x1, waiting for transfers between devices, on_device(): gradient = lax.psum(local_terms, 'af')  200 us
    ppermute x12, starting transfers between devices, padded_2(): lax.ppermute(tail, axis, [(i, (i + 1) % count) for i in range(ends)])  52.2 us
  transfers between devices with their start and end apart: 25, of which 12 were waited for; matrix products, arithmetic and copies ran while one was open for 1% of the time, Pallas kernels for 0%

commit v1 on v0

--- a/solution.py
+++ b/solution.py
@@ -79,7 +79,7 @@
     norm_now = squares(resid)
     for sweep in range(ITERS):
         image = adjoint(forward(direction)) + weights * direction
-        alpha = norm_now / lax.psum(inner(direction, image), ("gx", "gy"))
+        alpha = norm_now / lax.psum(lax.psum(inner(direction, image), "gx"), "gy")
         field = field + expand(alpha) * direction
         resid = resid - expand(alpha) * image
         norm_next = squares(resid)

time: 1230 us -> 1000 us (0.81)
  blocking collectives: 882 us -> 681 us
  waiting for transfers between devices: 210 us -> 185 us
    psum x1 -> x4, blocking collectives: 290 us -> 104 us  [on_device(): alpha = norm_now / lax.psum(lax.psum(inner(direction, image), 'gx'), 'gy')]
    psum x1, waiting for transfers between devices: 200 us -> 175 us  [on_device(): gradient = lax.psum(local_terms, 'af')]
    psum x2, blocking collectives: 592 us -> 577 us  [squares(): return lax.psum(inner(values, values), ('gx', 'gy'))]
  transfers between devices with their start and end apart: 25 -> 25, of which waited for: 12 -> 12; matrix products, arithmetic and copies ran while one was open for 1% -> 2% of each run, Pallas kernels for 0% -> 0%
where the time goes in v1:
time: 1000 us
  blocking collectives  681 us (68%)
  waiting for transfers between devices  185 us (18%)
  starting transfers between devices  68.1 us (7%)
  other arithmetic  34.6 us (3%)
  local copies, waits for them, and re-layouts  18.4 us (2%)
  between operations  14.6 us (1%)
    psum x2, blocking collectives, squares(): return lax.psum(inner(values, values), ('gx', 'gy'))  577 us
    psum x1, waiting for transfers between devices, on_device(): gradient = lax.psum(local_terms, 'af')  175 us
    psum x4, blocking collectives, on_device(): alpha = norm_now / lax.psum(lax.psum(inner(direction, image), 'gx'), 'gy')  104 us
    ppermute x12, starting transfers between devices, padded_2(): lax.ppermute(tail, axis, [(i, (i + 1) % count) for i in range(ends)])  52.6 us
  transfers between devices with their start and end apart: 25, of which 12 were waited for; matrix products, arithmetic and copies ran while one was open for 2% of the time, Pallas kernels for 0%

profile of v1, /device:TPU:1, one launch (start us, length us, event | category | flops | bytes accessed | tf_op | source)
XLA Modules:
  0.0 1002.1 jit_solution(7153647552932762608)
XLA Ops:
  7.2 0.9 fusion.80
  8.2 1.3 collective-permute-start
  9.6 4.8 collective-permute-start.1
  14.4 2.8 copy.48
  17.5 2.8 fusion.79
  20.3 1.8 fusion.48
  22.2 0.7 pad_maximum_fusion.62
  22.9 1.3 collective-permute-start.2
  24.1 4.0 collective-permute-start.3
  28.4 0.9 copy.58
  29.3 1.4 collective-permute-done.3
  30.7 7.4 fusion.45
  38.2 1.3 collective-permute-start.4
  39.5 4.0 collective-permute-start.5
  43.5 0.8 fusion.77
  44.3 0.5 collective-permute-done.5
  44.8 1.3 collective-permute-start.6
  46.1 4.3 collective-permute-start.7
  50.8 1.1 collective-permute-done.7
  51.9 2.1 fusion.38
  54.2 1.3 collective-permute-start.8
  55.5 4.6 collective-permute-start.9
  60.1 0.7 fusion.76
  60.8 0.5 collective-permute-done.9
  61.4 1.3 collective-permute-start.10
  62.7 4.9 collective-permute-start.11
  68.1 1.1 collective-permute-done.11
  69.2 4.1 multiply_reduce_fusion.1
  73.3 27.1 %psum.50 = f32[2]{0:T(128)S(1)} all-reduce(f32[2]{0:T(128)S(1)} %get-tuple-element.6), channel_id=1, replica_groups=mesh['gx'=8,'gy'=16,'af'=2] {'gx'}, use_global_device_ids=true, to_apply=%region_3.4 | all-reduce | flops 2 | bytes 16 | tf_op jit(solution)/shard_map/psum | solution.py:82
  100.3 32.5 %psum.51 = f32[2]{0:T(128)S(1)} all-reduce(f32[2]{0:T(128)S(1)} %psum.50), channel_id=1, replica_groups=mesh['gx'=8,'gy'=16,'af'=2] {'gy'}, use_global_device_ids=true, to_apply=%region_4.5 | all-reduce | flops 2 | bytes 16 | tf_op jit(solution)/shard_map/psum | solution.py:82
  132.8 290.5 %psum.49 = f32[2]{0:T(128)S(1)} all-reduce(f32[2]{0:T(128)S(1)} %get-tuple-element.7), channel_id=1, replica_groups=mesh['gx'=8,'gy'=16,'af'=2] {'gx','gy'}, use_global_device_ids=true, to_apply=%region_1.2 | all-reduce | flops 2 | bytes 16 | tf_op jit(solution)/shard_map/psum | solution.py:76
  423.3 2.1 multiply_reduce_fusion
  425.4 287.0 %psum.52 = f32[2]{0:T(128)S(1)} all-reduce(f32[2]{0:T(128)S(1)} %multiply_reduce_fusion), channel_id=1, replica_groups=mesh['gx'=8,'gy'=16,'af'=2] {'gx','gy'}, use_global_device_ids=true, to_apply=%region_6.7 | all-reduce | flops 2 | bytes 16 | tf_op jit(solution)/shard_map/psum | solution.py:76
  712.4 2.2 multiply_add_fusion.1
  714.7 1.3 collective-permute-start.12
  716.0 4.2 collective-permute-start.13
  720.1 0.7 fusion.73
  721.3 1.3 collective-permute-start.14
  722.6 4.2 collective-permute-start.15
  727.3 1.1 collective-permute-done.15
  728.3 2.0 fusion.25
  730.4 1.3 collective-permute-start.16
  731.7 4.6 collective-permute-start.17
  736.4 0.7 fusion.71
  737.1 0.5 collective-permute-done.17
  737.7 1.3 collective-permute-start.18
  739.0 4.9 collective-permute-start.19
  744.3 1.5 collective-permute-done.19
  745.8 3.0 fusion.19
  748.8 17.2 %psum.53 = f32[2]{0:T(128)S(1)} all-reduce(f32[2]{0:T(128)S(1)} %fusion.19), channel_id=1, replica_groups=mesh['gx'=8,'gy'=16,'af'=2] {'gx'}, use_global_device_ids=true, to_apply=%region_8.9 | all-reduce | flops 2 | bytes 16 | tf_op jit(solution)/shard_map/psum | solution.py:82
  766.0 26.8 %psum.54 = f32[2]{0:T(128)S(1)} all-reduce(f32[2]{0:T(128)S(1)} %psum.53), channel_id=1, replica_groups=mesh['gx'=8,'gy'=16,'af'=2] {'gy'}, use_global_device_ids=true, to_apply=%region_9.10 | all-reduce | flops 2 | bytes 16 | tf_op jit(solution)/shard_map/psum | solution.py:82
  792.9 2.2 multiply_add_fusion
  795.5 0.7 fusion.69
  796.3 1.3 collective-permute-start.20
  797.6 4.0 collective-permute-start.21
  801.8 1.1 collective-permute-done.21
  802.9 1.3 collective-permute-start.22
  804.2 4.1 collective-permute-start.23
  808.8 1.1 collective-permute-done.23
  809.8 2.7 fusion.10
  812.5 1.4 fusion.62
  814.0 4.1 copy.70
  818.1 175.1 %all-reduce.14.cloned.1.call-done = f32[32,32,128]{2,0,1:T(8,128)} async-done(((f32[32,32,128]{2,0,1:T(8,128)}), f32[32,32,128]{2,0,1:T(8,128)}) %all-reduce.14.cloned.1.call-update) | async-done | bytes 524304 | tf_op jit(solution)/shard_map/psum | solution.py:94
  993.2 2.1 copy.71
  (56 shorter events, 4.5 us)
Async XLA Ops:
  7.2 986.0 %all-reduce.14.cloned.1.call-start = ((), (), s32[]{:S(2)}) async-start(), calls=%async_computation | async-start | bytes 1048576 | tf_op jit(solution)/shard_map/psum | solution.py:94
  8.2 14.0 %collective-permute-start = (f32[2,2,1,32,128]{4,2,3,0,1:T(1,128)S(1)}, f32[2,2,1,32,128]{4,2,3,0,1:T(1,128)S(1)}, u32[]{:S(2)}, u32[]{:S(2)}) collective-permute-start(f32[2,2,1,32,128]{4,2,3,0,1:T(1,128)S(1)} %copy.50), channel_id=1, source_target_pairs={{32,0},{64,32},{96,64},{128,96},{160,128},{192,160},{224,192},{33,... | collective-permute-start | bytes 196616 | tf_op jit(solution)/shard_map/ppermute | solution.py:21
  9.6 7.6 copy-start.5
  9.6 7.6 copy-start.4
  9.6 12.6 %collective-permute-start.1 = (f32[2,2,1,32,128]{4,2,3,0,1:T(1,128)S(1)}, f32[2,2,1,32,128]{4,2,3,0,1:T(1,128)S(1)}, u32[]{:S(2)}, u32[]{:S(2)}) collective-permute-start(f32[2,2,1,32,128]{4,2,3,0,1:T(1,128)S(1)} %copy.52), channel_id=1, source_target_pairs={{0,32},{32,64},{64,96},{96,128},{128,160},{160,192},{192,224},{1,3... | collective-permute-start | bytes 196616 | tf_op jit(solution)/shard_map/ppermute | solution.py:19
  17.2 5.0 copy-start.2
  20.3 1.8 copy-start.6
  22.9 6.4 collective-permute-start.2
  24.1 6.6 collective-permute-start.3
  38.2 6.1 collective-permute-start.4
  39.5 5.3 collective-permute-start.5
  44.8 6.0 collective-permute-start.6
  46.1 5.8 collective-permute-start.7
  54.2 6.7 collective-permute-start.8
  55.5 5.9 collective-permute-start.9
  61.4 6.6 collective-permute-start.10
  62.7 6.5 collective-permute-start.11
  714.6 31.3 %copy-start.1 = (f32[2,2,32,32,128]{4,2,3,0,1:T(8,128)}, f32[2,2,32,32,128]{4,2,3,0,1:T(8,128)S(1)}, u32[]{:S(2)}) copy-start(f32[2,2,32,32,128]{4,2,3,0,1:T(8,128)S(1)} %multiply_add_fusion.1) | copy-start | bytes 6291460
  714.7 6.2 collective-permute-start.12
  716.0 5.3 collective-permute-start.13
  721.3 5.9 collective-permute-start.14
  722.6 5.7 collective-permute-start.15
  730.4 6.7 collective-permute-start.16
  731.7 5.9 collective-permute-start.17
  737.7 6.6 collective-permute-start.18
  739.0 6.8 collective-permute-start.19
  795.0 17.5 %copy-start = (f32[2,2,32,32,128]{4,2,3,0,1:T(8,128)}, f32[2,2,32,32,128]{4,2,3,0,1:T(8,128)S(1)}, u32[]{:S(2)}) copy-start(f32[2,2,32,32,128]{4,2,3,0,1:T(8,128)S(1)} %multiply_add_fusion) | copy-start | bytes 6291460
  796.3 5.5 collective-permute-start.20
  797.6 5.3 collective-permute-start.21
  802.9 5.8 collective-permute-start.22
  804.2 5.6 copy-start.3
  804.2 5.6 collective-permute-start.23
Sparse Core Ops, SparseCore 0:
  814.1 179.0 all-reduce.13
